TPU v7x, 32 devices: a whole 2x2x4 slice. The times are simulated.
32 devices in a mesh: row: 4 (over x, core), col: 2 (over y), depth: 4 (over z).
Axes of the slice: x: 2, y: 2, z: 4, core: 2. Of those that a mesh axis runs over, the one named last changes fastest.
Arguments:
- tokens: bfloat16 [2048, 8192], P('col', ('row', 'depth')), may hold values from -6 to 6
- weight: bfloat16 [8192, 24576], P(('row', 'depth'), 'col'), may hold values from -0.0625 to 0.0625
- prev_tokens: bfloat16 [2048, 8192], P('col', ('row', 'depth')), may hold values from -6 to 6
- prev_grad: bfloat16 [2048, 24576], P(('row', 'depth'), 'col'), may hold values from -0.3125 to 0.3125
Outputs:
- qkv: bfloat16 [2048, 24576], P(('row', 'depth'), 'col')
- weight_grad: float32 [8192, 24576], P(('row', 'depth'), 'col')
All inputs are finite; a program needn't handle non-finite values.
Results may differ from a plain program's by a relative error of at most 0.001.
Values may be sent and summed in bfloat16 or wider, within the bound.
No kernel may reach another device: no remote copies, remote signals or barrier semaphores. Data moves between devices by JAX's collectives and lax.ppermute only.
A program may use at most 256 MiB of HBM per device.

v0:
```python
import jax
import jax.numpy as jnp
from jax import lax
from jax.sharding import PartitionSpec as P


def local(tokens, weight, prev_tokens, prev_grad):
    gathered, prev_gathered = (
        lax.all_gather(tokens, "col", axis=0, tiled=True),
        lax.all_gather(prev_tokens, "col", axis=0, tiled=True),
    )
    summed = lax.psum_scatter(
        jnp.dot(gathered, weight, preferred_element_type=jnp.float32),
        ("row", "depth"),
        scatter_dimension=0,
        tiled=True,
    )
    qkv = summed.astype(jnp.bfloat16)
    weight_grad = lax.dot_general(
        prev_gathered,
        lax.all_gather(prev_grad, ("row", "depth"), axis=0, tiled=True),
        (((0,), (0,)), ((), ())),
        preferred_element_type=jnp.float32,
    )
    return (qkv, weight_grad)


def solution(mesh):
    placed = (
        P("col", ("row", "depth")),
        P(("row", "depth"), "col"),
        P("col", ("row", "depth")),
        P(("row", "depth"), "col"),
    )
    return jax.shard_map(
        local,
        mesh=mesh,
        in_specs=placed,
        out_specs=(P(("row", "depth"), "col"), P(("row", "depth"), "col")),
        check_vma=False,
    )
```

profile of v0, /device:TPU:0, one launch (start us, length us, event | category | flops | bytes accessed | tf_op | source)
XLA Modules:
  0.0 1262.4 jit_solution(6793693843953948556)
XLA Ops:
  7.2 0.0 all-gather.4.cloned.1.call-start
  7.2 0.7 all-gather.4.cloned.1.call-update
  7.9 0.0 all-gather.6.cloned.1.call-start
  7.9 0.7 all-gather.6.cloned.1.call-update
  8.6 0.0 all-gather.8.cloned.1.call-start
  8.7 0.7 all-gather.8.cloned.1.call-update
  9.4 0.0 reduce-scatter.4.cloned.1.call-start
  9.4 35.9 %all-gather.4.cloned.1.call-done = bf16[2048,512]{1,0:T(8,128)(2,1)} async-done(((bf16[1024,512]{1,0:T(8,128)(2,1)}), bf16[2048,512]{1,0:T(8,128)(2,1)}) %all-gather.4.cloned.1.call-update) | async-done | bytes 2097168 | tf_op jit(solution)/shard_map/all_gather | solution.py:9
  45.4 44.9 %fusion = f32[2048,12288]{1,0:T(8,128)} fusion(bf16[2048,512]{1,0:T(8,128)(2,1)} %all-gather.4.cloned.1.call-done, bf16[512,12288]{1,0:T(8,128)(2,1)} %param.5), kind=kOutput, calls=%fused_computation | convolution fusion | flops 25769803776 | bytes 115343360 | tf_op jit(solution)/shard_map/dot_general | solution.py:13
  90.3 0.0 reduce-scatter.4.cloned.1.call-update
  90.3 0.0 all-gather.6.cloned.1.call-done
  90.3 253.4 %all-gather.8.cloned.1.call-done = bf16[2048,12288]{1,0:T(8,128)(2,1)} async-done(((bf16[128,12288]{1,0:T(8,128)(2,1)}), bf16[2048,12288]{1,0:T(8,128)(2,1)}) %all-gather.8.cloned.1.call-update) | async-done | bytes 50331664 | tf_op jit(solution)/shard_map/all_gather | solution.py:21
  343.7 44.9 %fusion.1 = f32[512,12288]{1,0:T(8,128)} fusion(bf16[2048,512]{1,0:T(8,128)(2,1)} %all-gather.6.cloned.1.call-done, bf16[2048,12288]{1,0:T(8,128)(2,1)} %all-gather.8.cloned.1.call-done), kind=kOutput, calls=%fused_computation.1 | convolution fusion | flops 25769803776 | bytes 77594624 | tf_op jit(solution)/shard_map/dot_general | solution.py:19
  388.7 862.3 %reduce-scatter.4.cloned.1.call-done = f32[128,12288]{1,0:T(8,128)} async-done(((f32[2048,12288]{1,0:T(8,128)}), f32[128,12288]{1,0:T(8,128)}) %reduce-scatter.4.cloned.1.call-update) | async-done | bytes 6291472
  1251.0 4.8 convert_element_type.3
Async XLA Ops:
  7.2 38.2 %all-gather.4.cloned.1.call-start = ((), (), s32[]{:S(2)}) async-start(), calls=%async_computation.1 | async-start | bytes 3145728 | tf_op jit(solution)/shard_map/all_gather | solution.py:9
  7.9 82.4 %all-gather.6.cloned.1.call-start = ((), (), s32[]{:S(2)}) async-start(), calls=%async_computation.2 | async-start | bytes 3145728 | tf_op jit(solution)/shard_map/all_gather | solution.py:10
  8.6 335.1 %all-gather.8.cloned.1.call-start = ((), (), s32[]{:S(2)}) async-start(), calls=%async_computation.3 | async-start | bytes 53477376 | tf_op jit(solution)/shard_map/all_gather | solution.py:21
  9.4 1241.6 %reduce-scatter.4.cloned.1.call-start = ((), (), s32[]{:S(2)}) async-start(), calls=%async_computation.4 | async-start | bytes 106954752
Sparse Core Ops, SparseCore 0:
  9.5 35.8 all-gather.3
  46.9 33.0 all-gather.5
  81.6 262.1 all-gather.7
  347.8 903.1 reduce-scatter.3
where the time goes:
time: 1260 us
  waiting for transfers between devices  1150 us (91%)
  matrix products  89.9 us (7%)
  between operations  13.8 us (1%)
    unnamed x5, waiting for transfers between devices  864 us
    all_gather x1, waiting for transfers between devices, local(): lax.all_gather(prev_grad, ('row', 'depth'), axis=0, tiled=True)  253 us
    dot_general x1, matrix products, local(): lax.dot_general(prev_gathered, lax.all_gather(prev_grad, ('row', 'depth')...  44.9 us
    dot_general x1, matrix products, local(): jnp.dot(gathered, weight, preferred_element_type=jnp.float32)  44.9 us
    all_gather x1, waiting for transfers between devices, local(): lax.all_gather(tokens, 'col', axis=0, tiled=True)  35.9 us
  transfers between devices with their start and end apart: 4, of which 3 were waited for; matrix products, arithmetic and copies ran while one was open for 7% of the time, Pallas kernels for 0%

commit v1 on v0

v1 whole, which is shorter than its diff:
```python
import jax
import jax.numpy as jnp
from jax import lax
from jax.sharding import PartitionSpec as P

CORES = 2


def make_local(row_size, chunks):
    high = row_size // CORES

    def moved(shift):
        return [(h * CORES + c, ((h + shift) % high) * CORES + c) for h in range(high) for c in range(CORES)]

    swap = [(h * CORES + c, h * CORES + 1 - c) for h in range(high) for c in range(CORES)]

    def over_chips(block):
        return jnp.concatenate([block] + [lax.ppermute(block, "row", moved(s)) for s in range(1, high)], axis=0)

    def orders():
        r = lax.axis_index("row")
        h, c = r // CORES, r % CORES
        return [[((h + high - s) % high) * CORES + k for s in range(high)] for k in (c, 1 - c)]

    def picked(array, axis, width, order):
        return jnp.concatenate([lax.dynamic_slice_in_dim(array, i * width, width, axis) for i in order], axis=axis)

    def local(tokens, weight, prev_tokens, prev_grad):
        own, other = orders()
        k_width = weight.shape[0]
        step = weight.shape[1] // chunks

        prev_rows = lax.all_gather(prev_grad, "depth", axis=0, tiled=True)
        pieces = [weight[:, i * step:(i + 1) * step] for i in range(chunks)]
        paired = [over_chips(piece) for piece in pieces]

        full = lax.all_gather(tokens, "col", axis=0, tiled=True)
        mine = lax.all_to_all(full, "row", split_axis=0, concat_axis=1, tiled=True)
        t_own = picked(mine, 1, k_width, own)
        t_other = picked(mine, 1, k_width, other)

        summed = []
        for pair in paired:
            across = lax.ppermute(pair, "row", swap)
            partial = jnp.dot(t_own, pair, preferred_element_type=jnp.float32)
            partial = partial + jnp.dot(t_other, across, preferred_element_type=jnp.float32)
            out = lax.psum_scatter(partial, "depth", scatter_dimension=0, tiled=True)
            summed.append(out.astype(jnp.bfloat16))
        qkv = jnp.concatenate(summed, axis=1)

        prev_full = lax.all_gather(prev_tokens, "col", axis=0, tiled=True)
        height = prev_full.shape[0] // row_size
        g_own = over_chips(prev_rows)
        g_other = lax.ppermute(g_own, "row", swap)
        contract = (((0,), (0,)), ((), ()))
        weight_grad = lax.dot_general(
            picked(prev_full, 0, height, own), g_own, contract, preferred_element_type=jnp.float32
        ) + lax.dot_general(
            picked(prev_full, 0, height, other), g_other, contract, preferred_element_type=jnp.float32
        )
        return (qkv, weight_grad)

    return local


def solution(mesh):
    placed = (
        P("col", ("row", "depth")),
        P(("row", "depth"), "col"),
        P("col", ("row", "depth")),
        P(("row", "depth"), "col"),
    )
    return jax.shard_map(
        make_local(mesh.shape["row"], 4),
        mesh=mesh,
        in_specs=placed,
        out_specs=(P(("row", "depth"), "col"), P(("row", "depth"), "col")),
        check_vma=False,
    )
```

time: 1260 us -> 846 us (0.67)
  waiting for transfers between devices: 1150 us -> 657 us
  local copies, waits for them, and re-layouts: 0 us -> 37 us
  other arithmetic: 4.82 us -> 20.7 us
    unnamed x5 -> x7, waiting for transfers between devices: 864 us -> 2.12 us
    ppermute x0 -> x10, waiting for transfers between devices: none -> 490 us  [the longest x5 460 us: over_chips(): lax.ppermute(block, 'row', moved(s))]
    all_gather x3, waiting for transfers between devices: 289 us -> 36.2 us  [the longest x1 36.2 us: local(): prev_rows = lax.all_gather(prev_grad, 'depth', axis=0, tiled=True)]
    reduce_scatter x0 -> x4, waiting for transfers between devices: none -> 104 us  [local(): out = lax.psum_scatter(partial, 'depth', scatter_dimension=0, tiled=True)]
    all_to_all x0 -> x1, waiting for transfers between devices: none -> 24.9 us  [local(): mine = lax.all_to_all(full, 'row', split_axis=0, concat_axis=1, tiled=True)]
    concatenate x0 -> x5, other arithmetic: none -> 14.3 us  [the longest x4 12.5 us: over_chips(): jnp.concatenate([block] + [lax.ppermute(block, 'row', moved(s)) for s in...]
    dot_general x2 -> x10, matrix products: 89.9 us -> 97.3 us  [the longest x1 29.9 us: local(): lax.dot_general(picked(prev_full, 0, height, own), g_own, contract, prefe...]
  transfers between devices with their start and end apart: 4 -> 18, of which waited for: 3 -> 11; matrix products, arithmetic and copies ran while one was open for 7% -> 12% of each run, Pallas kernels for 0% -> 0%
where the time goes in v1:
time: 846 us; the launch traced here: 837 us
  waiting for transfers between devices  657 us (78%)
  matrix products  97.3 us (12%)
  local copies, waits for them, and re-layouts  37 us (4%)
  other arithmetic  20.7 us (2%)
  between operations  14.9 us (2%)
  starting transfers between devices  10.6 us (1%)
    ppermute x5, waiting for transfers between devices, over_chips(): lax.ppermute(block, 'row', moved(s))  460 us
    reduce_scatter x4, waiting for transfers between devices, local(): out = lax.psum_scatter(partial, 'depth', scatter_dimension=0, tiled=True)  104 us
    all_gather x1, waiting for transfers between devices, local(): prev_rows = lax.all_gather(prev_grad, 'depth', axis=0, tiled=True)  36.2 us
    dot_general x1, matrix products, local(): lax.dot_general(picked(prev_full, 0, height, own), g_own, contract, prefe...  29.9 us
    ppermute x4, waiting for transfers between devices, local(): across = lax.ppermute(pair, 'row', swap)  29.8 us
    dot_general x4, matrix products, local(): partial = jnp.dot(t_own, pair, preferred_element_type=jnp.float32)  27.8 us
    all_to_all x1, waiting for transfers between devices, local(): mine = lax.all_to_all(full, 'row', split_axis=0, concat_axis=1, tiled=True)  24.9 us
    dot_general x1, matrix products, local(): lax.dot_general(picked(prev_full, 0, height, other), g_other, contract, p...  23.5 us
  transfers between devices with their start and end apart: 18, of which 11 were waited for; matrix products, arithmetic and copies ran while one was open for 12% of the time, Pallas kernels for 0%

profile of v1, /device:TPU:0, one launch (start us, length us, event | category | flops | bytes accessed | tf_op | source)
XLA Modules:
  0.0 837.5 jit_solution(12760932070385451466)
XLA Ops:
  7.2 0.7 all-gather.4.cloned.1.call-update
  7.9 0.7 all-gather.8.cloned.1.call-update
  8.6 8.6 %fusion.13 = (bf16[512,3072]{1,0:T(8,128)(2,1)S(1)}, bf16[512,3072]{1,0:T(8,128)(2,1)}, bf16[512,3072]{1,0:T(8,128)(2,1)}, bf16[512,3072]{1,0:T(8,128)(2,1)}) fusion(bf16[512,12288]{1,0:T(8,128)(2,1)} %param.5), kind=kLoop, calls=%fused_computation.35 | loop fusion | bytes 25165824 | tf_op jit(solution)/shard_map/slice | solution.py:34
  17.3 3.0 collective-permute-start
  20.2 68.1 %collective-permute-done = bf16[512,3072]{1,0:T(8,128)(2,1)S(1)} collective-permute-done((bf16[512,3072]{1,0:T(8,128)(2,1)S(1)}, bf16[512,3072]{1,0:T(8,128)(2,1)S(1)}, u32[]{:S(2)}, u32[]{:S(2)}) %collective-permute-start) | collective-permute-done | bytes 3145760 | tf_op jit(solution)/shard_map/ppermute | solution.py:18
  88.3 3.4 pad_maximum_fusion
  91.8 0.2 copy-done.4
  92.0 3.6 all-to-all-start
  95.6 0.7 all-gather.6.cloned.1.call-update
  96.4 24.9 %all-to-all-done = bf16[4,512,512]{2,1,0:T(8,128)(2,1)S(1)} async-done(((bf16[4,512,512]{2,1,0:T(8,128)(2,1)}), bf16[4,512,512]{2,1,0:T(8,128)(2,1)S(1)}, u32[]{:S(2)}, u32[]{:S(2)}) %all-to-all-start) | async-done | bytes 2097184 | tf_op jit(solution)/shard_map/all_to_all | solution.py:38
  121.3 2.4 copy.6
  123.7 1.7 constant_dynamic-slice_fusion.7
  125.4 5.7 fusion.12
  131.1 5.4 convolution_add_fusion.4
  136.6 0.4 collective-permute-start.2
  136.9 69.7 %collective-permute-done.2 = bf16[512,3072]{1,0:T(8,128)(2,1)S(1)} collective-permute-done((bf16[512,3072]{1,0:T(8,128)(2,1)}, bf16[512,3072]{1,0:T(8,128)(2,1)S(1)}, u32[]{:S(2)}, u32[]{:S(2)}) %collective-permute-start.2) | collective-permute-done | bytes 3145760 | tf_op jit(solution)/shard_map/ppermute | solution.py:18
  206.6 2.3 pad_maximum_fusion.1
  209.0 10.1 %collective-permute-done.3 = bf16[1024,3072]{1,0:T(8,128)(2,1)S(1)} collective-permute-done((bf16[1024,3072]{1,0:T(8,128)(2,1)S(1)}, bf16[1024,3072]{1,0:T(8,128)(2,1)S(1)}, u32[]{:S(2)}, u32[]{:S(2)}) %collective-permute-start.3) | collective-permute-done | bytes 6291488 | tf_op jit(solution)/shard_map/ppermute | solution.py:44
  219.2 3.5 fusion.11
  222.7 5.4 convolution_add_fusion.3
  228.1 0.2 reduce-scatter.9.cloned.1.call-start
  228.3 0.6 collective-permute-start.4
  229.0 36.2 %all-gather.8.cloned.1.call-done = bf16[512,12288]{1,0:T(8,128)(2,1)} async-done(((bf16[128,12288]{1,0:T(8,128)(2,1)}), bf16[512,12288]{1,0:T(8,128)(2,1)}) %all-gather.8.cloned.1.call-update) | async-done | bytes 12582928 | tf_op jit(solution)/shard_map/all_gather | solution.py:33
  265.1 1.5 collective-permute-start.8
  266.6 33.1 %collective-permute-done.4 = bf16[512,3072]{1,0:T(8,128)(2,1)} collective-permute-done((bf16[512,3072]{1,0:T(8,128)(2,1)}, bf16[512,3072]{1,0:T(8,128)(2,1)}, u32[]{:S(2)}, u32[]{:S(2)}) %collective-permute-start.4) | collective-permute-done | bytes 3145760 | tf_op jit(solution)/shard_map/ppermute | solution.py:18
  299.7 3.3 pad_maximum_fusion.2
  303.1 0.6 collective-permute-start.6
  303.7 9.5 %collective-permute-done.5 = bf16[1024,3072]{1,0:T(8,128)(2,1)S(1)} collective-permute-done((bf16[1024,3072]{1,0:T(8,128)(2,1)S(1)}, bf16[1024,3072]{1,0:T(8,128)(2,1)S(1)}, u32[]{:S(2)}, u32[]{:S(2)}) %collective-permute-start.5) | collective-permute-done | bytes 6291488 | tf_op jit(solution)/shard_map/ppermute | solution.py:44
  313.2 3.5 fusion.10
  316.7 8.0 convolution_add_fusion.2
  324.7 0.3 reduce-scatter.11.cloned.1.call-start
  325.0 10.7 %constant_dynamic-update-slice_fusion.1 = bf16[1024,12288]{1,0:T(8,128)(2,1)} fusion(bf16[512,12288]{1,0:T(8,128)(2,1)} %all-gather.8.cloned.1.call-done), kind=kLoop, calls=%fused_computation.20 | loop fusion | bytes 25165824
  335.7 233.7 %collective-permute-done.8 = bf16[512,12288]{1,0:T(8,128)(2,1)} collective-permute-done((bf16[512,12288]{1,0:T(8,128)(2,1)}, bf16[512,12288]{1,0:T(8,128)(2,1)}, u32[]{:S(2)}, u32[]{:S(2)}) %collective-permute-start.8) | collective-permute-done | bytes 12582944 | tf_op jit(solution)/shard_map/ppermute | solution.py:18
  569.3 10.7 %constant_dynamic-update-slice_fusion = bf16[1024,12288]{1,0:T(8,128)(2,1)} fusion(bf16[1024,12288]{1,0:T(8,128)(2,1)} %constant_dynamic-update-slice_fusion.1, bf16[512,12288]{1,0:T(8,128)(2,1)} %collective-permute-done.8), kind=kLoop, calls=%fused_computation.19 | loop fusion | bytes 25165824 | tf_op jit(solution)/shard_map/concatenate | solution.py:18
  580.0 55.9 %collective-permute-done.6 = bf16[512,3072]{1,0:T(8,128)(2,1)} collective-permute-done((bf16[512,3072]{1,0:T(8,128)(2,1)}, bf16[512,3072]{1,0:T(8,128)(2,1)}, u32[]{:S(2)}, u32[]{:S(2)}) %collective-permute-start.6) | collective-permute-done | bytes 3145760 | tf_op jit(solution)/shard_map/ppermute | solution.py:18
  635.9 3.4 pad_maximum_fusion.3
  639.4 10.1 %collective-permute-done.7 = bf16[1024,3072]{1,0:T(8,128)(2,1)S(1)} collective-permute-done((bf16[1024,3072]{1,0:T(8,128)(2,1)S(1)}, bf16[1024,3072]{1,0:T(8,128)(2,1)S(1)}, u32[]{:S(2)}, u32[]{:S(2)}) %collective-permute-start.7) | collective-permute-done | bytes 6291488 | tf_op jit(solution)/shard_map/ppermute | solution.py:44
  649.6 3.5 fusion.9
  653.0 9.0 %convolution_add_fusion.1 = f32[512,3072]{1,0:T(8,128)} fusion(f32[512,3072]{1,0:T(8,128)S(1)} %fusion.9, bf16[512,512]{0,1:T(8,128)(2,1)S(1)} %get-tuple-element.13, bf16[512,512]{0,1:T(8,128)(2,1)S(1)} %get-tuple-element.10, bf16[512,3072]{1,0:T(8,128)(2,1)} %collective-permute-done.6, bf16[512,3072]{1,0:T(8,128)(2,1)} %get-tuple-element.4), kind=kOutput, calls=%fused_computation.5 | convolution fusion | flops 3237478400 | bytes 19922944 | tf_op jit(solution)/shard_map/dot_general | solution.py:45
  662.1 2.7 constant_dynamic-slice_fusion.3
  664.8 1.5 convert_element_type.12
  666.4 1.5 convert_element_type.13
  667.9 2.0 convert_element_type.14
  669.9 103.7 %reduce-scatter.11.cloned.1.call-done = f32[128,3072]{1,0:T(8,128)} async-done(((f32[512,3072]{1,0:T(8,128)}), f32[128,3072]{1,0:T(8,128)}) %reduce-scatter.11.cloned.1.call-update) | async-done | bytes 1572880 | tf_op jit(solution)/shard_map/reduce_scatter | solution.py:47
  773.5 1.5 convert_element_type.15
  775.0 1.8 pad_maximum_fusion.4
  776.8 23.5 %fusion.3 = f32[512,12288]{1,0:T(8,128)} fusion(bf16[1024,12288]{1,0:T(8,128)(2,1)} %collective-permute-done.9, bf16[512,512]{1,0:T(8,128)(2,1)} %get-tuple-element.7, bf16[512,512]{1,0:T(8,128)(2,1)} %get-tuple-element.8), kind=kOutput, calls=%fused_computation.15 | convolution fusion | flops 12886999040 | bytes 51380224 | tf_op jit(solution)/shard_map/dot_general | solution.py:58
  800.3 29.9 %convolution_add_fusion = f32[512,12288]{1,0:T(8,128)} fusion(f32[512,12288]{1,0:T(8,128)} %fusion.3, bf16[1024,12288]{1,0:T(8,128)(2,1)} %constant_dynamic-update-slice_fusion, bf16[512,512]{1,0:T(8,128)(2,1)S(1)} %get-tuple-element.9, bf16[512,512]{1,0:T(8,128)(2,1)S(1)} %get-tuple-element.6), kind=kOutput, calls=%fused_computation | convolution fusion | flops 12893290496 | bytes 76546048 | tf_op jit(solution)/shard_map/dot_general | solution.py:56
  (32 shorter events, 0.6 us)
Async XLA Ops:
  7.2 84.8 %all-gather.4.cloned.1.call-start = ((), (), s32[]{:S(2)}) async-start(), calls=%async_computation.5 | async-start | bytes 3145728 | tf_op jit(solution)/shard_map/all_gather | solution.py:37
  7.9 257.2 %all-gather.8.cloned.1.call-start = ((), (), s32[]{:S(2)}) async-start(), calls=%async_computation.11 | async-start | bytes 15728640 | tf_op jit(solution)/shard_map/all_gather | solution.py:33
  17.3 74.5 %copy-start.2 = (bf16[512,3072]{1,0:T(8,128)(2,1)}, bf16[512,3072]{1,0:T(8,128)(2,1)S(1)}, u32[]{:S(2)}) copy-start(bf16[512,3072]{1,0:T(8,128)(2,1)S(1)} %get-tuple-element.2) | copy-start | bytes 9437188
  17.3 71.1 %collective-permute-start = (bf16[512,3072]{1,0:T(8,128)(2,1)S(1)}, bf16[512,3072]{1,0:T(8,128)(2,1)S(1)}, u32[]{:S(2)}, u32[]{:S(2)}) collective-permute-start(bf16[512,3072]{1,0:T(8,128)(2,1)S(1)} %get-tuple-element.2), channel_id=1, source_target_pairs={{0,16},{8,24},{16,0},{24,8},{1,17},{9,25},{17,1},{25,9},{2,18},{10... | collective-permute-start | bytes 9437192 | tf_op jit(solution)/shard_map/ppermute | solution.py:18
  88.3 3.6 copy-start.4
  92.0 33.4 %collective-permute-start.1 = (bf16[1024,3072]{1,0:T(8,128)(2,1)}, bf16[1024,3072]{1,0:T(8,128)(2,1)}, u32[]{:S(2)}, u32[]{:S(2)}) collective-permute-start(bf16[1024,3072]{1,0:T(8,128)(2,1)} %pad_maximum_fusion), channel_id=1, source_target_pairs={{0,8},{8,0},{16,24},{24,16},{1,9},{9,1},{17,25},{25,17},{2,10},{10... | collective-permute-start | bytes 18874376 | tf_op jit(solution)/shard_map/ppermute | solution.py:44
  92.0 29.4 %all-to-all-start = ((bf16[4,512,512]{2,1,0:T(8,128)(2,1)}), bf16[4,512,512]{2,1,0:T(8,128)(2,1)S(1)}, u32[]{:S(2)}, u32[]{:S(2)}) async-start(bf16[4,512,512]{2,1,0:T(8,128)(2,1)} %bitcast.11), calls=%async_computation | async-start | bytes 4194304 | tf_op jit(solution)/shard_map/all_to_all | solution.py:38
  95.6 566.5 %all-gather.6.cloned.1.call-start = ((), (), s32[]{:S(2)}) async-start(), calls=%async_computation.10 | async-start | bytes 3145728 | tf_op jit(solution)/shard_map/all_gather | solution.py:51
  96.3 568.5 %reduce-scatter.5.cloned.1.call-start = ((), (), s32[]{:S(2)}) async-start(), calls=%async_computation.6 | async-start | bytes 7864320 | tf_op jit(solution)/shard_map/reduce_scatter | solution.py:47
  125.4 5.8 copy-start.3
  125.4 5.8 copy-start.5
  136.5 529.8 %reduce-scatter.7.cloned.1.call-start = ((), (), s32[]{:S(2)}) async-start(), calls=%async_computation.7 | async-start | bytes 7864320 | tf_op jit(solution)/shard_map/reduce_scatter | solution.py:47
  136.6 70.0 %collective-permute-start.2 = (bf16[512,3072]{1,0:T(8,128)(2,1)}, bf16[512,3072]{1,0:T(8,128)(2,1)S(1)}, u32[]{:S(2)}, u32[]{:S(2)}) collective-permute-start(bf16[512,3072]{1,0:T(8,128)(2,1)} %get-tuple-element.3), channel_id=1, source_target_pairs={{0,16},{8,24},{16,0},{24,8},{1,17},{9,25},{17,1},{25,9},{2,18},{10... | collective-permute-start | bytes 9437192 | tf_op jit(solution)/shard_map/ppermute | solution.py:18
  208.9 13.7 %copy-start.1 = (bf16[512,3072]{1,0:T(8,128)(2,1)S(1)}, bf16[512,3072]{1,0:T(8,128)(2,1)}, u32[]{:S(2)}) copy-start(bf16[512,3072]{1,0:T(8,128)(2,1)} %get-tuple-element.3) | copy-start | bytes 9437188
  208.9 10.2 %collective-permute-start.3 = (bf16[1024,3072]{1,0:T(8,128)(2,1)S(1)}, bf16[1024,3072]{1,0:T(8,128)(2,1)S(1)}, u32[]{:S(2)}, u32[]{:S(2)}) collective-permute-start(bf16[1024,3072]{1,0:T(8,128)(2,1)S(1)} %pad_maximum_fusion.1), channel_id=1, source_target_pairs={{0,8},{8,0},{16,24},{24,16},{1,9},{9,1},{17,25},{25,17},{2,10},{10... | collective-permute-start | bytes 18874376 | tf_op jit(solution)/shard_map/ppermute | solution.py:44
  228.1 439.8 %reduce-scatter.9.cloned.1.call-start = ((), (), s32[]{:S(2)}) async-start(), calls=%async_computation.8 | async-start | bytes 7864320 | tf_op jit(solution)/shard_map/reduce_scatter | solution.py:47
  228.3 71.4 %collective-permute-start.4 = (bf16[512,3072]{1,0:T(8,128)(2,1)}, bf16[512,3072]{1,0:T(8,128)(2,1)}, u32[]{:S(2)}, u32[]{:S(2)}) collective-permute-start(bf16[512,3072]{1,0:T(8,128)(2,1)} %get-tuple-element.5), channel_id=1, source_target_pairs={{0,16},{8,24},{16,0},{24,8},{1,17},{9,25},{17,1},{25,9},{2,18},{10... | collective-permute-start | bytes 9437192 | tf_op jit(solution)/shard_map/ppermute | solution.py:18
  265.1 304.2 %collective-permute-start.8 = (bf16[512,12288]{1,0:T(8,128)(2,1)}, bf16[512,12288]{1,0:T(8,128)(2,1)}, u32[]{:S(2)}, u32[]{:S(2)}) collective-permute-start(bf16[512,12288]{1,0:T(8,128)(2,1)} %all-gather.8.cloned.1.call-done), channel_id=1, source_target_pairs={{0,16},{8,24},{16,0},{24,8},{1,17},{9,25},{17,1},{25,9},{2,18},{10... | collective-permute-start | bytes 37748744 | tf_op jit(solution)/shard_map/ppermute | solution.py:18
  303.0 10.2 %collective-permute-start.5 = (bf16[1024,3072]{1,0:T(8,128)(2,1)S(1)}, bf16[1024,3072]{1,0:T(8,128)(2,1)S(1)}, u32[]{:S(2)}, u32[]{:S(2)}) collective-permute-start(bf16[1024,3072]{1,0:T(8,128)(2,1)S(1)} %pad_maximum_fusion.2), channel_id=1, source_target_pairs={{0,8},{8,0},{16,24},{24,16},{1,9},{9,1},{17,25},{25,17},{2,10},{10... | collective-permute-start | bytes 18874376 | tf_op jit(solution)/shard_map/ppermute | solution.py:44
  303.0 13.6 %copy-start = (bf16[512,3072]{1,0:T(8,128)(2,1)S(1)}, bf16[512,3072]{1,0:T(8,128)(2,1)}, u32[]{:S(2)}) copy-start(bf16[512,3072]{1,0:T(8,128)(2,1)} %get-tuple-element.5) | copy-start | bytes 9437188
  303.1 332.8 %collective-permute-start.6 = (bf16[512,3072]{1,0:T(8,128)(2,1)}, bf16[512,3072]{1,0:T(8,128)(2,1)}, u32[]{:S(2)}, u32[]{:S(2)}) collective-permute-start(bf16[512,3072]{1,0:T(8,128)(2,1)} %get-tuple-element.4), channel_id=1, source_target_pairs={{0,16},{8,24},{16,0},{24,8},{1,17},{9,25},{17,1},{25,9},{2,18},{10... | collective-permute-start | bytes 9437192 | tf_op jit(solution)/shard_map/ppermute | solution.py:18
  324.7 448.8 %reduce-scatter.11.cloned.1.call-start = ((), (), s32[]{:S(2)}) async-start(), calls=%async_computation.9 | async-start | bytes 7864320 | tf_op jit(solution)/shard_map/reduce_scatter | solution.py:47
  580.0 196.8 %collective-permute-start.9 = (bf16[1024,12288]{1,0:T(8,128)(2,1)}, bf16[1024,12288]{1,0:T(8,128)(2,1)}, u32[]{:S(2)}, u32[]{:S(2)}) collective-permute-start(bf16[1024,12288]{1,0:T(8,128)(2,1)} %constant_dynamic-update-slice_fusion), channel_id=1, source_target_pairs={{0,8},{8,0},{16,24},{24,16},{1,9},{9,1},{17,25},{25,17},{2,10},{10... | collective-permute-start | bytes 75497480 | tf_op jit(solution)/shard_map/ppermute | solution.py:54
  639.3 10.2 %collective-permute-start.7 = (bf16[1024,3072]{1,0:T(8,128)(2,1)S(1)}, bf16[1024,3072]{1,0:T(8,128)(2,1)S(1)}, u32[]{:S(2)}, u32[]{:S(2)}) collective-permute-start(bf16[1024,3072]{1,0:T(8,128)(2,1)S(1)} %pad_maximum_fusion.3), channel_id=1, source_target_pairs={{0,8},{8,0},{16,24},{24,16},{1,9},{9,1},{17,25},{25,17},{2,10},{10... | collective-permute-start | bytes 18874376 | tf_op jit(solution)/shard_map/ppermute | solution.py:44
Sparse Core Ops, SparseCore 0:
  9.5 35.8 all-gather.3
  46.9 218.1 all-gather.7
  266.7 31.2 all-gather.5
  300.2 110.7 reduce-scatter.4
  413.1 111.2 reduce-scatter.6
  526.6 111.2 reduce-scatter.8
  662.2 111.2 reduce-scatter.10
